TPU v7x, 32 devices: a whole 2x2x4 slice. The times are simulated.
32 devices in a mesh: island: 2 (over core), dp: 4 (over z), tensor: 4 (over y, x).
Axes of the slice: x: 2, y: 2, z: 4, core: 2. Of those that a mesh axis runs over, the one named last changes fastest.
Arguments:
- pseudo_grad: float32 [2, 48, 256, 5120], P('island', None, 'dp', 'tensor'), may hold values from -1000 to 1000, as said below
- block_owner: int32 [48], replicated, may hold values from 0 to 7, as said below
Outputs:
- update: bfloat16 [8, 12, 256, 5120], P(('island', 'dp'), None, None, 'tensor')
Inputs may be any that keep to these rules, and one draw needn't show every extreme that they name: `pseudo_grad`: float pseudo-gradients; entries lie within the range. `block_owner`: every owner holds at most 12 blocks and at least one; some owner holds exactly 12.
All inputs are finite; a program needn't handle non-finite values.
Results may differ from a plain program's by a relative error of at most 0.001.
Values sent between devices are 32-bit elements; how exact they have to be, the bound alone decides.
A program may use at most 128 MiB of HBM per device.

v0:
```python
import functools
import math

import jax
import jax.numpy as jnp
from jax import lax
from jax.experimental import pallas as pl
from jax.experimental.pallas import tpu as pltpu
from jax.sharding import PartitionSpec as P

COEF_A = 3.4445
COEF_B = -4.775
COEF_C = 2.0315
EPSILON = 1e-07


def rank_before(key):
    positions = jnp.arange(key.shape[0], dtype=jnp.int32)
    same = (key[None, :] == key[:, None]) & (positions[None, :] < positions[:, None])
    return jnp.sum(same.astype(jnp.int32), axis=1)


def invert(target, count):
    positions = jnp.arange(target.shape[0], dtype=jnp.int32)
    matches = target[None, :] == jnp.arange(count, dtype=jnp.int32)[:, None]
    return jnp.sum(jnp.where(matches, positions[None, :], 0), axis=1), jnp.any(matches, axis=1)


def pack_kernel(group, index_ref, half_ref, *refs):
    out_ref = refs[-1]
    for g in range(group):
        out_ref[g] = refs[2 * g][0] + refs[2 * g + 1][0]


def pack(own_grad, other, index, island):
    count = index.shape[0]
    rows, half = other.shape[1], other.shape[2]
    group = max(g for g in range(1, 7) if count % g == 0)
    specs = []
    for g in range(group):
        specs.append(pl.BlockSpec((1, rows, half), lambda i, ix, h, g=g: (ix[i * group + g], 0, h[0])))
        specs.append(pl.BlockSpec((1, rows, half), lambda i, ix, h, g=g: (ix[i * group + g], 0, 0)))
    return pl.pallas_call(
        functools.partial(pack_kernel, group),
        grid_spec=pltpu.PrefetchScalarGridSpec(
            num_scalar_prefetch=2,
            grid=(count // group,),
            in_specs=specs,
            out_specs=pl.BlockSpec((group, rows, half), lambda i, ix, h: (i, 0, 0)),
        ),
        out_shape=jax.ShapeDtypeStruct((count, rows, half), jnp.float32),
        compiler_params=pltpu.CompilerParams(vmem_limit_bytes=48 * 2**20),
    )(index, island.reshape(1), *([own_grad, other] * group))


def split(value):
    high = value.astype(jnp.bfloat16)
    return high, (value - high.astype(jnp.float32)).astype(jnp.bfloat16)


def dot(left, right, axis=0):
    dims = (((1,), (axis,)), ((), ()))
    return lax.dot_general(left, right, dims, preferred_element_type=jnp.float32)


def product(left, right):
    left_high, left_low = split(left)
    right_high, right_low = split(right)
    return dot(left_high, right_high) + (dot(left_high, right_low) + dot(left_low, right_high))


def factor_of(gram):
    on_diagonal = lax.broadcasted_iota(jnp.int32, gram.shape, 0) == lax.broadcasted_iota(jnp.int32, gram.shape, 1)
    squares = jnp.sum(jnp.where(on_diagonal, gram, 0.0), axis=(0, 1), keepdims=True)
    inverse = 1.0 / (jnp.sqrt(squares) + EPSILON)
    scaled_identity = jnp.where(on_diagonal, COEF_A, 0.0)
    start = gram * (inverse * inverse)
    first = scaled_identity + (COEF_B * start + COEF_C * product(start, start))
    second_gram = product(product(first, start), first)
    second = scaled_identity + (COEF_B * second_gram + COEF_C * product(second_gram, second_gram))
    return product(second, first) * inverse


def transport_kernel(
    n, tensors, chunk, chunks, send_ref, a_ref, b_ref, m_ref,
    stage, block, gram, gram_in, part, part_in, total, factor,
    local_sem, out_sem, send_sem, recv_sem, relay_send, relay_recv,
    gram_send, gram_recv, part_send, part_recv, total_send, total_recv,
):
    me = lax.axis_index("dp")
    island = lax.axis_index("island")
    tensor = lax.axis_index("tensor")
    partner = 1 - island
    mesh_ids = pl.DeviceIdType.MESH
    barrier = pltpu.get_barrier_semaphore()
    for d in range(1, n):
        pl.semaphore_signal(barrier, inc=1, device_id={"dp": lax.rem(me + d, n)}, device_id_type=mesh_ids)
    for d in range(1, tensors):
        pl.semaphore_signal(barrier, inc=1, device_id={"tensor": lax.rem(tensor + d, tensors)}, device_id_type=mesh_ids)
    pl.semaphore_signal(barrier, inc=1, device_id={"island": partner}, device_id_type=mesh_ids)
    pl.semaphore_wait(barrier, n + tensors - 1)

    size = gram.shape[1]
    mid = size // 2
    own_rows = pl.ds(pl.multiple_of(island * mid, mid), mid)
    partner_rows = pl.ds(pl.multiple_of(partner * mid, mid), mid)

    def span(c):
        return pl.ds(c * chunk, chunk)

    def remote(c, d):
        peer = lax.rem(me + d, n)
        return pltpu.make_async_remote_copy(
            src_ref=send_ref.at[peer, span(c)],
            dst_ref=a_ref.at[span(c), me],
            send_sem=send_sem.at[c, d],
            recv_sem=recv_sem.at[c, d],
            device_id={"dp": peer},
            device_id_type=mesh_ids,
        )

    def to_partner(source, target, send, recv):
        return pltpu.make_async_remote_copy(
            src_ref=source, dst_ref=target, send_sem=send, recv_sem=recv,
            device_id={"island": partner}, device_id_type=mesh_ids,
        )

    def relay(c):
        return to_partner(a_ref.at[span(c)], b_ref.at[span(c)], relay_send.at[c], relay_recv.at[c])

    def gram_copy(c):
        return to_partner(gram.at[span(c), partner_rows], gram_in.at[span(c)], gram_send.at[c], gram_recv.at[c])

    def total_copy(c):
        rows = total.at[span(c), own_rows]
        return to_partner(rows, rows, total_send.at[c], total_recv.at[c])

    def part_copy(c, d):
        return pltpu.make_async_remote_copy(
            src_ref=part.at[span(c)],
            dst_ref=part_in.at[d - 1, span(c)],
            send_sem=part_send.at[c, d],
            recv_sem=part_recv.at[c, d],
            device_id={"tensor": lax.rem(tensor + d, tensors)},
            device_id_type=mesh_ids,
        )

    def factor_copy(c):
        return pltpu.make_async_copy(factor.at[span(c)], m_ref.at[span(c)], out_sem.at[c])

    def start(c, carry):
        for d in range(1, n):
            remote(c, d).start()
        return carry

    lax.fori_loop(0, chunks, start, 0)
    load = pltpu.make_async_copy(send_ref.at[me], stage, local_sem.at[0])
    load.start()
    load.wait()
    store = pltpu.make_async_copy(stage, a_ref.at[pl.ds(0, chunk * chunks), me], local_sem.at[1])
    store.start()
    store.wait()

    def arrive(c, carry):
        for d in range(1, n):
            remote(c, d).wait_recv()
        relay(c).start()
        fetch = pltpu.make_async_copy(a_ref.at[span(c)], block, local_sem.at[2])
        fetch.start()
        fetch.wait()

        def own_gram(k, inner):
            high, low = split(block[k].reshape(size, block.shape[3]))
            cross = dot(high, low, 1)
            gram[c * chunk + k] = dot(high, high, 1) + (cross + cross.T)
            return inner

        lax.fori_loop(0, chunk, own_gram, 0)
        gram_copy(c).start()
        gram_copy(c).wait_recv()
        part[span(c)] = gram[span(c), own_rows] + gram_in[span(c)]
        for d in range(1, tensors):
            part_copy(c, d).start()
        for d in range(1, tensors):
            part_copy(c, d).wait_recv()
        summed = part[span(c)]
        for d in range(1, tensors):
            summed = summed + part_in[d - 1, span(c)]
        total[span(c), own_rows] = summed
        total_copy(c).start()
        total_copy(c).wait_recv()

        def own_factor(k, inner):
            factor[c * chunk + k] = factor_of(total[c * chunk + k])
            return inner

        lax.fori_loop(0, chunk, own_factor, 0)
        factor_copy(c).start()
        return carry

    lax.fori_loop(0, chunks, arrive, 0)

    def finish(c, carry):
        for d in range(1, n):
            remote(c, d).wait_send()
        for d in range(1, tensors):
            part_copy(c, d).wait_send()
        relay(c).wait()
        gram_copy(c).wait_send()
        total_copy(c).wait_send()
        factor_copy(c).wait()
        return carry

    lax.fori_loop(0, chunks, finish, 0)


def transport(send, most, chunk, tensors, collective_id):
    n, count, rows, half = send.shape
    chunks = count // chunk
    size = n * rows
    shape = jax.ShapeDtypeStruct((most, n, rows, half), jnp.float32)
    anywhere = pl.BlockSpec(memory_space=pl.ANY)
    one_each = pltpu.SemaphoreType.DMA((chunks,))
    return pl.pallas_call(
        functools.partial(transport_kernel, n, tensors, chunk, chunks),
        out_shape=(shape, shape, jax.ShapeDtypeStruct((most, size, size), jnp.float32)),
        in_specs=[anywhere],
        out_specs=(anywhere, anywhere, anywhere),
        scratch_shapes=[
            pltpu.VMEM((count, rows, half), jnp.float32),
            pltpu.VMEM((chunk, n, rows, half), jnp.float32),
            pltpu.VMEM((count, size, size), jnp.float32),
            pltpu.VMEM((count, size // 2, size), jnp.float32),
            pltpu.VMEM((count, size // 2, size), jnp.float32),
            pltpu.VMEM((tensors - 1, count, size // 2, size), jnp.float32),
            pltpu.VMEM((count, size, size), jnp.float32),
            pltpu.VMEM((count, size, size), jnp.float32),
            pltpu.SemaphoreType.DMA((3,)),
            one_each,
            pltpu.SemaphoreType.DMA((chunks, n)),
            pltpu.SemaphoreType.DMA((chunks, n)),
            one_each,
            one_each,
            one_each,
            one_each,
            pltpu.SemaphoreType.DMA((chunks, tensors)),
            pltpu.SemaphoreType.DMA((chunks, tensors)),
            one_each,
            one_each,
        ],
        compiler_params=pltpu.CompilerParams(
            collective_id=collective_id, has_side_effects=True, vmem_limit_bytes=60 * 2**20
        ),
    )(send)


def final_kernel(scale, place_ref, valid_ref, island_ref, m_ref, a_ref, b_ref, out_ref):
    half = a_ref.shape[2]
    valid = valid_ref[pl.program_id(0)] > 0
    island = island_ref[0]
    for source, part in ((a_ref, island), (b_ref, 1 - island)):
        value = scale * product(m_ref[0], source[0])
        columns = pl.ds(pl.multiple_of(part * half, half), half)
        out_ref[0, 0, :, columns] = jnp.where(valid, value, 0.0).astype(jnp.bfloat16)


def finals(factor, mine, partner, place, valid, island, width):
    count = place.shape[0]
    size, half = mine.shape[1], mine.shape[2]
    pick = lambda i, p, v, h: (p[i], 0, 0)
    return pl.pallas_call(
        functools.partial(final_kernel, math.sqrt(width)),
        grid_spec=pltpu.PrefetchScalarGridSpec(
            num_scalar_prefetch=3,
            grid=(count,),
            in_specs=[
                pl.BlockSpec((1, size, size), pick),
                pl.BlockSpec((1, size, half), pick),
                pl.BlockSpec((1, size, half), pick),
            ],
            out_specs=pl.BlockSpec((1, 1, size, 2 * half), lambda i, p, v, h: (0, i, 0, 0)),
        ),
        out_shape=jax.ShapeDtypeStruct((1, count, size, 2 * half), jnp.bfloat16),
        compiler_params=pltpu.CompilerParams(vmem_limit_bytes=48 * 2**20),
    )(place, valid.astype(jnp.int32), island.reshape(1), factor, mine, partner)


def body(pseudo_grad, block_owner):
    own_grad = pseudo_grad[0]
    blocks, rows, columns = own_grad.shape
    half = columns // 2
    dp_count = lax.axis_size("dp")
    island_count = lax.axis_size("island")
    tensors = lax.axis_size("tensor")
    owner_count = island_count * dp_count
    slot_count = 2 * (blocks // owner_count)
    most = island_count * slot_count
    least = blocks // dp_count
    chunk = max(1, slot_count // 4)
    island = lax.axis_index("island")
    device_dp = lax.axis_index("dp")

    slot = rank_before(block_owner)
    chip = lax.rem(block_owner, dp_count)
    chip_slot = rank_before(chip)
    send_index, _ = invert(chip * most + chip_slot, dp_count * most)
    send_index = send_index.reshape(dp_count, most)
    needed = jnp.max(chip_slot) + 1
    own_index, own_valid = invert(block_owner * slot_count + slot, owner_count * slot_count)
    base = (island * dp_count + device_dp) * slot_count
    own_block = lax.dynamic_slice_in_dim(own_index, base, slot_count)
    own_valid = lax.dynamic_slice_in_dim(own_valid, base, slot_count)
    own_place = chip_slot[own_block]

    theirs = lax.dynamic_slice_in_dim(own_grad, (1 - island) * half, half, axis=2)
    other = lax.ppermute(theirs, "island", [(0, 1), (1, 0)])

    counts = [c for c in range(chunk, most + 1, chunk) if c >= least]

    def branch(count, number):
        def run(own_grad, other):
            packed = pack(own_grad, other, send_index[:, :count].reshape(-1), island)
            return transport(packed.reshape(dp_count, count, rows, half), most, chunk, tensors, number)
        return run

    choice = jnp.sum((needed > jnp.array(counts, dtype=jnp.int32)).astype(jnp.int32))
    mine, partner, factor = lax.switch(choice, [branch(c, i) for i, c in enumerate(counts)], own_grad, other)
    mine = mine.reshape(most, dp_count * rows, half)
    partner = partner.reshape(most, dp_count * rows, half)
    return finals(factor, mine, partner, own_place, own_valid, island, columns * tensors)


def solution(mesh):
    in_specs = (P("island", None, "dp", "tensor"), P())
    out_specs = P(("island", "dp"), None, None, "tensor")
    return jax.shard_map(body, mesh=mesh, in_specs=in_specs, out_specs=out_specs, check_vma=False)
```

profile of v0, /device:TPU:9, one launch (start us, length us, event | category | flops | bytes accessed | tf_op | source)
XLA Modules:
  0.0 367.7 jit_solution(13120651731472373144)
XLA Ops:
  0.0 0.0 copy-start.1
  0.0 0.0 copy-start
  0.0 7.4 %dynamic-slice_bitcast_fusion = f32[48,64,640]{2,1,0:T(8,128)} fusion(f32[1,48,64,1280]{3,2,1,0:T(8,128)} %param.8, s32[]{:T(128)S(6)} %select_n.21), kind=kLoop, calls=%fused_computation.1 | loop fusion | bytes 15728644 | tf_op jit(solution)/shard_map/dynamic_slice | solution.py:315
  7.4 0.7 collective-permute-start
  8.1 0.0 copy-done
  8.1 0.2 convert_reduce_fusion
  8.3 0.2 convert_reduce_fusion.1
  8.4 0.7 multiply_add_fusion
  9.7 0.0 copy-done.1
  9.7 0.7 fusion.3
  11.0 0.1 select_reduce_fusion.1
  11.1 0.1 compare_select_fusion
  11.2 0.7 gather_fusion
  11.8 0.1 fusion
  11.9 0.1 dynamic-slice_convert_fusion.valid_ref
  12.0 0.1 select_reduce_fusion
  12.1 8.3 %collective-permute-done = f32[48,64,640]{2,1,0:T(8,128)} collective-permute-done((f32[48,64,640]{2,1,0:T(8,128)}, f32[48,64,640]{2,1,0:T(8,128)}, u32[]{:S(2)}, u32[]{:S(2)}) %collective-permute-start) | collective-permute-done | bytes 7864352 | tf_op jit(solution)/shard_map/ppermute | solution.py:316
  20.4 332.1 %conditional.1 = (f32[24,256,256]{2,1,0:T(8,128)}, f32[24,256,640]{2,1,0:T(8,128)}, f32[24,256,640]{2,1,0:T(8,128)}) conditional(s32[]{:T(128)} %clamp.3, (s32[96]{0:T(128)S(1)}, s32[]{:T(128)}, f32[48,64,1280]{2,1,0:T(8,128)}, f32[48,64,640]{2,1,0:T(8,128)}) %tuple.44, (s32[96]{0:T(128)S(1)}, s32[]{:T(128)}, ...), branch_computations={%region_7.8_spmd, %region_8.9_spmd, %region_9.10_spmd, %region_10.... | conditional | bytes 1464 | solution.py:327
  20.4 0.1 reshape.70
  20.5 0.1 reshape.71.index_ref
  20.6 15.7 %branch_2_fun.2 = f32[72,64,640]{2,1,0:T(8,128)} custom-call(s32[72]{0:T(128)S(1)} %reshape.71.index_ref, s32[1]{0:T(128)} %bitcast.8.half_ref, f32[48,64,1280]{2,1,0:T(8,128)} %get-tuple-element.82.refs_0_.refs_2_.refs_4_.refs_6_.refs_8_.refs_10_, f32[48,64,640]{2,1,0:T(8,128)} %get-tuple-element.83.refs_1_.refs_3_.refs_5_.refs_7_.refs_9_.refs_11_, ...), custom_call_target="tpu_custom_call" | custom-call | tf_op jit(solution)/shard_map/cond/branch_2_fun/pallas_call | solution.py:43
  36.3 316.3 %branch_2_fun.3 = (f32[24,4,64,640]{3,2,1,0:T(8,128)}, f32[24,4,64,640]{3,2,1,0:T(8,128)}, f32[24,256,256]{2,1,0:T(8,128)}) custom-call(f32[4,18,64,640]{3,2,1,0:T(8,128)} %bitcast.35), custom_call_target="tpu_custom_call" | custom-call | tf_op jit(solution)/shard_map/cond/branch_2_fun/pallas_call | solution.py:224
  352.6 15.2 %shard_map.37 = bf16[1,12,256,1280]{3,2,1,0:T(8,128)(2,1)} custom-call(s32[12]{0:T(128)S(1)} %gather_fusion, s32[12]{0:T(128)S(1)} %dynamic-slice_convert_fusion.valid_ref, s32[1]{0:T(128)} %bitcast.20.island_ref, f32[24,256,256]{2,1,0:T(8,128)} %get-tuple-element.104.m_ref, f32[24,256,640]{2,1,0:T(8,128)} %get-tuple-element.105.a_ref, ...), custom_call_target="tpu_custom_call" | custom-call | tf_op jit(solution)/shard_map/pallas_call | solution.py:271
  (2 shorter events, 0.0 us)
Async XLA Ops:
  0.0 9.7 %copy-start.1 = (s32[5]{0:T(128)S(1)}, s32[5]{0:T(128)}, u32[]{:S(2)}) copy-start(s32[5]{0:T(128)} %constant.42.clone) | copy-start | bytes 64
  0.0 8.1 %copy-start = (s32[48]{0:T(128)S(1)}, s32[48]{0:T(128)}, u32[]{:S(2)}) copy-start(s32[48]{0:T(128)} %param.9) | copy-start | bytes 580
  7.4 13.1 %collective-permute-start = (f32[48,64,640]{2,1,0:T(8,128)}, f32[48,64,640]{2,1,0:T(8,128)}, u32[]{:S(2)}, u32[]{:S(2)}) collective-permute-start(f32[48,64,640]{2,1,0:T(8,128)} %dynamic-slice_bitcast_fusion), channel_id=1, source_target_pairs={{0,16},{16,0},{1,17},{17,1},{2,18},{18,2},{3,19},{19,3},{4,20},{20... | collective-permute-start | bytes 23592968 | tf_op jit(solution)/shard_map/ppermute | solution.py:316
where the time goes:
time: 369 us; the launch traced here: 368 us
  Pallas kernels  347 us (94%)
  waiting for transfers between devices  8.33 us (2%)
  local copies, waits for them, and re-layouts  8.22 us (2%)
    pallas_call x1, Pallas kernels, transport(): pl.pallas_call(functools.partial(transport_kernel, n, tensors, chunk, chu...  316 us
    pallas_call x1, Pallas kernels, pack(): pl.pallas_call(functools.partial(pack_kernel, group), grid_spec=pltpu.Pre...  15.7 us
    pallas_call x1, Pallas kernels, finals(): pl.pallas_call(functools.partial(final_kernel, math.sqrt(width)), grid_sp...  15.2 us
    ppermute x1, waiting for transfers between devices, body(): other = lax.ppermute(theirs, 'island', [(0, 1), (1, 0)])  8.33 us
    dynamic_slice x1, local copies, waits for them, and re-layouts, body(): lax.dynamic_slice_in_dim(own_grad, (1 - island) * half, half, axis=2)  7.39 us
  transfers between devices with their start and end apart: 1, of which 1 were waited for; matrix products, arithmetic and copies ran while one was open for 1% of the time, Pallas kernels for 0%

commit v1 on v0

--- a/solution.py
+++ b/solution.py
@@ -66,7 +66,9 @@
 def product(left, right):
     left_high, left_low = split(left)
     right_high, right_low = split(right)
-    return dot(left_high, right_high) + (dot(left_high, right_low) + dot(left_low, right_high))
+    stacked_left = jnp.concatenate([left_high, left_high, left_low], axis=1)
+    stacked_right = jnp.concatenate([right_high, right_low, right_high], axis=0)
+    return dot(stacked_left, stacked_right)
 
 
 def factor_of(gram):
@@ -79,6 +81,44 @@
     second_gram = product(product(first, start), first)
     second = scaled_identity + (COEF_B * second_gram + COEF_C * product(second_gram, second_gram))
     return product(second, first) * inverse
+
+
+def exchange_kernel(pieces, grad_ref, out_ref, send_sem, recv_sem):
+    partner = 1 - lax.axis_index("island")
+    half = out_ref.shape[2]
+    step = out_ref.shape[0] // pieces
+    barrier = pltpu.get_barrier_semaphore()
+    pl.semaphore_signal(barrier, inc=1, device_id={"island": partner}, device_id_type=pl.DeviceIdType.MESH)
+    pl.semaphore_wait(barrier, 1)
+    columns = pl.ds(pl.multiple_of(partner * half, half), half)
+    copies = [
+        pltpu.make_async_remote_copy(
+            src_ref=grad_ref.at[pl.ds(p * step, step), :, columns],
+            dst_ref=out_ref.at[pl.ds(p * step, step)],
+            send_sem=send_sem.at[p],
+            recv_sem=recv_sem.at[p],
+            device_id={"island": partner},
+            device_id_type=pl.DeviceIdType.MESH,
+        )
+        for p in range(pieces)
+    ]
+    for copy in copies:
+        copy.start()
+    for copy in copies:
+        copy.wait()
+
+
+def exchange(own_grad):
+    blocks, rows, columns = own_grad.shape
+    pieces = 4 if blocks % 4 == 0 else 1
+    return pl.pallas_call(
+        functools.partial(exchange_kernel, pieces),
+        out_shape=jax.ShapeDtypeStruct((blocks, rows, columns // 2), jnp.float32),
+        in_specs=[pl.BlockSpec(memory_space=pl.ANY)],
+        out_specs=pl.BlockSpec(memory_space=pl.ANY),
+        scratch_shapes=[pltpu.SemaphoreType.DMA((pieces,)), pltpu.SemaphoreType.DMA((pieces,))],
+        compiler_params=pltpu.CompilerParams(collective_id=100, has_side_effects=True),
+    )(own_grad)
 
 
 def transport_kernel(
@@ -105,16 +145,30 @@
     own_rows = pl.ds(pl.multiple_of(island * mid, mid), mid)
     partner_rows = pl.ds(pl.multiple_of(partner * mid, mid), mid)
 
+    def steps(run):
+        bulk = chunks - 1
+
+        def whole(c, carry):
+            run((c, c * chunk, chunk))
+            return carry
+
+        def single(j, carry):
+            run((bulk + j, bulk * chunk + j, 1))
+            return carry
+
+        lax.fori_loop(0, bulk, whole, 0)
+        lax.fori_loop(0, chunk, single, 0)
+
     def span(c):
-        return pl.ds(c * chunk, chunk)
+        return pl.ds(c[1], c[2])
 
     def remote(c, d):
         peer = lax.rem(me + d, n)
         return pltpu.make_async_remote_copy(
             src_ref=send_ref.at[peer, span(c)],
             dst_ref=a_ref.at[span(c), me],
-            send_sem=send_sem.at[c, d],
-            recv_sem=recv_sem.at[c, d],
+            send_sem=send_sem.at[c[0], d],
+            recv_sem=recv_sem.at[c[0], d],
             device_id={"dp": peer},
             device_id_type=mesh_ids,
         )
@@ -126,34 +180,33 @@
         )
 
     def relay(c):
-        return to_partner(a_ref.at[span(c)], b_ref.at[span(c)], relay_send.at[c], relay_recv.at[c])
+        return to_partner(a_ref.at[span(c)], b_ref.at[span(c)], relay_send.at[c[0]], relay_recv.at[c[0]])
 
     def gram_copy(c):
-        return to_partner(gram.at[span(c), partner_rows], gram_in.at[span(c)], gram_send.at[c], gram_recv.at[c])
+        return to_partner(gram.at[span(c), partner_rows], gram_in.at[span(c)], gram_send.at[c[0]], gram_recv.at[c[0]])
 
     def total_copy(c):
         rows = total.at[span(c), own_rows]
-        return to_partner(rows, rows, total_send.at[c], total_recv.at[c])
+        return to_partner(rows, rows, total_send.at[c[0]], total_recv.at[c[0]])
 
     def part_copy(c, d):
         return pltpu.make_async_remote_copy(
             src_ref=part.at[span(c)],
             dst_ref=part_in.at[d - 1, span(c)],
-            send_sem=part_send.at[c, d],
-            recv_sem=part_recv.at[c, d],
+            send_sem=part_send.at[c[0], d],
+            recv_sem=part_recv.at[c[0], d],
             device_id={"tensor": lax.rem(tensor + d, tensors)},
             device_id_type=mesh_ids,
         )
 
     def factor_copy(c):
-        return pltpu.make_async_copy(factor.at[span(c)], m_ref.at[span(c)], out_sem.at[c])
-
-    def start(c, carry):
+        return pltpu.make_async_copy(factor.at[span(c)], m_ref.at[span(c)], out_sem.at[c[0]])
+
+    def start(c):
         for d in range(1, n):
             remote(c, d).start()
-        return carry
-
-    lax.fori_loop(0, chunks, start, 0)
+
+    steps(start)
     load = pltpu.make_async_copy(send_ref.at[me], stage, local_sem.at[0])
     load.start()
     load.wait()
@@ -161,21 +214,21 @@
     store.start()
     store.wait()
 
-    def arrive(c, carry):
+    def arrive(c):
         for d in range(1, n):
             remote(c, d).wait_recv()
         relay(c).start()
-        fetch = pltpu.make_async_copy(a_ref.at[span(c)], block, local_sem.at[2])
+        fetch = pltpu.make_async_copy(a_ref.at[span(c)], block.at[pl.ds(0, c[2])], local_sem.at[2])
         fetch.start()
         fetch.wait()
 
         def own_gram(k, inner):
             high, low = split(block[k].reshape(size, block.shape[3]))
             cross = dot(high, low, 1)
-            gram[c * chunk + k] = dot(high, high, 1) + (cross + cross.T)
+            gram[c[1] + k] = dot(high, high, 1) + (cross + cross.T)
             return inner
 
-        lax.fori_loop(0, chunk, own_gram, 0)
+        lax.fori_loop(0, c[2], own_gram, 0)
         gram_copy(c).start()
         gram_copy(c).wait_recv()
         part[span(c)] = gram[span(c), own_rows] + gram_in[span(c)]
@@ -191,16 +244,15 @@
         total_copy(c).wait_recv()
 
         def own_factor(k, inner):
-            factor[c * chunk + k] = factor_of(total[c * chunk + k])
+            factor[c[1] + k] = factor_of(total[c[1] + k])
             return inner
 
-        lax.fori_loop(0, chunk, own_factor, 0)
+        lax.fori_loop(0, c[2], own_factor, 0)
         factor_copy(c).start()
-        return carry
-
-    lax.fori_loop(0, chunks, arrive, 0)
-
-    def finish(c, carry):
+
+    steps(arrive)
+
+    def finish(c):
         for d in range(1, n):
             remote(c, d).wait_send()
         for d in range(1, tensors):
@@ -209,9 +261,8 @@
         gram_copy(c).wait_send()
         total_copy(c).wait_send()
         factor_copy(c).wait()
-        return carry
-
-    lax.fori_loop(0, chunks, finish, 0)
+
+    steps(finish)
 
 
 def transport(send, most, chunk, tensors, collective_id):
@@ -220,7 +271,7 @@
     size = n * rows
     shape = jax.ShapeDtypeStruct((most, n, rows, half), jnp.float32)
     anywhere = pl.BlockSpec(memory_space=pl.ANY)
-    one_each = pltpu.SemaphoreType.DMA((chunks,))
+    one_each = pltpu.SemaphoreType.DMA((chunks - 1 + chunk,))
     return pl.pallas_call(
         functools.partial(transport_kernel, n, tensors, chunk, chunks),
         out_shape=(shape, shape, jax.ShapeDtypeStruct((most, size, size), jnp.float32)),
@@ -237,14 +288,14 @@
             pltpu.VMEM((count, size, size), jnp.float32),
             pltpu.SemaphoreType.DMA((3,)),
             one_each,
-            pltpu.SemaphoreType.DMA((chunks, n)),
-            pltpu.SemaphoreType.DMA((chunks, n)),
-            one_each,
-            one_each,
-            one_each,
-            one_each,
-            pltpu.SemaphoreType.DMA((chunks, tensors)),
-            pltpu.SemaphoreType.DMA((chunks, tensors)),
+            pltpu.SemaphoreType.DMA((chunks - 1 + chunk, n)),
+            pltpu.SemaphoreType.DMA((chunks - 1 + chunk, n)),
+            one_each,
+            one_each,
+            one_each,
+            one_each,
+            pltpu.SemaphoreType.DMA((chunks - 1 + chunk, tensors)),
+            pltpu.SemaphoreType.DMA((chunks - 1 + chunk, tensors)),
             one_each,
             one_each,
         ],
@@ -312,8 +363,7 @@
     own_valid = lax.dynamic_slice_in_dim(own_valid, base, slot_count)
     own_place = chip_slot[own_block]
 
-    theirs = lax.dynamic_slice_in_dim(own_grad, (1 - island) * half, half, axis=2)
-    other = lax.ppermute(theirs, "island", [(0, 1), (1, 0)])
+    other = exchange(own_grad)
 
     counts = [c for c in range(chunk, most + 1, chunk) if c >= least]
 

time: 369 us -> 324 us (0.88)
  Pallas kernels: 347 us -> 316 us
  waiting for transfers between devices: 8.33 us -> 0 us
  local copies, waits for them, and re-layouts: 8.22 us -> 0.82 us
    pallas_call x1, Pallas kernels: 316 us -> 274 us  [transport(): pl.pallas_call(functools.partial(transport_kernel, n, tensors, chunk, chu...]
    pallas_call x0 -> x1, Pallas kernels: none -> 13.2 us  [exchange(): pl.pallas_call(functools.partial(exchange_kernel, pieces), out_shape=jax....]
    ppermute x1 -> x0, waiting for transfers between devices: 8.33 us -> none  [body(): other = lax.ppermute(theirs, 'island', [(0, 1), (1, 0)])]
    dynamic_slice x1 -> x0, local copies, waits for them, and re-layouts: 7.39 us -> none  [body(): lax.dynamic_slice_in_dim(own_grad, (1 - island) * half, half, axis=2)]
  transfers between devices with their start and end apart: 1 -> 0, of which waited for: 1 -> 0; matrix products, arithmetic and copies ran while one was open for 1% -> 0% of each run, Pallas kernels for 0% -> 0%
where the time goes in v1:
time: 324 us; the launch traced here: 322 us
  Pallas kernels  316 us (98%)
  other arithmetic  4.13 us (1%)
    pallas_call x1, Pallas kernels, transport(): pl.pallas_call(functools.partial(transport_kernel, n, tensors, chunk, chu...  274 us
    pallas_call x1, Pallas kernels, finals(): pl.pallas_call(functools.partial(final_kernel, math.sqrt(width)), grid_sp...  15.2 us
    pallas_call x1, Pallas kernels, pack(): pl.pallas_call(functools.partial(pack_kernel, group), grid_spec=pltpu.Pre...  13.2 us
    pallas_call x1, Pallas kernels, exchange(): pl.pallas_call(functools.partial(exchange_kernel, pieces), out_shape=jax....  13.2 us

profile of v1, /device:TPU:9, one launch (start us, length us, event | category | flops | bytes accessed | tf_op | source)
XLA Modules:
  0.0 322.2 jit_solution(7796217311104682385)
XLA Ops:
  0.0 0.9 convert_reduce_fusion
  0.9 0.7 multiply_add_fusion.1
  1.6 0.2 convert_reduce_fusion.1
  1.8 0.1 fusion
  1.9 0.1 select_reduce_fusion.1
  1.9 0.1 compare_select_fusion
  2.0 0.1 dynamic-slice_convert_fusion.valid_ref
  2.1 0.6 multiply_add_fusion
  3.4 1.3 fusion.3
  5.3 0.1 select_reduce_fusion
  5.4 0.7 gather_fusion
  6.1 13.2 %shard_map.37 = f32[48,64,640]{2,1,0:T(8,128)} custom-call(f32[48,64,1280]{2,1,0:T(8,128)} %bitcast.26), custom_call_target="tpu_custom_call" | custom-call | tf_op jit(solution)/shard_map/pallas_call | solution.py:114
  19.3 287.7 %conditional.1 = (f32[24,256,256]{2,1,0:T(8,128)}, f32[24,256,640]{2,1,0:T(8,128)}, f32[24,256,640]{2,1,0:T(8,128)}) conditional(s32[]{:T(128)} %clamp.3, (s32[96]{0:T(128)S(1)}, s32[]{:T(128)}, f32[48,64,1280]{2,1,0:T(8,128)}, f32[48,64,640]{2,1,0:T(8,128)}) %tuple.44, (s32[96]{0:T(128)S(1)}, s32[]{:T(128)}, ...), branch_computations={%region_7.8_spmd, %region_8.9_spmd, %region_9.10_spmd, %region_10.... | conditional | bytes 1464 | solution.py:377
  19.3 0.1 reshape.63
  19.4 0.1 reshape.64.index_ref
  19.5 13.2 %branch_1_fun.2 = f32[60,64,640]{2,1,0:T(8,128)} custom-call(s32[60]{0:T(128)S(1)} %reshape.64.index_ref, s32[1]{0:T(128)} %bitcast.4.half_ref, f32[48,64,1280]{2,1,0:T(8,128)} %get-tuple-element.75.refs_0_.refs_2_.refs_4_.refs_6_.refs_8_.refs_10_, f32[48,64,640]{2,1,0:T(8,128)} %get-tuple-element.76.refs_1_.refs_3_.refs_5_.refs_7_.refs_9_.refs_11_, ...), custom_call_target="tpu_custom_call" | custom-call | tf_op jit(solution)/shard_map/cond/branch_1_fun/pallas_call | solution.py:43
  32.7 274.1 %branch_1_fun.3 = (f32[24,4,64,640]{3,2,1,0:T(8,128)}, f32[24,4,64,640]{3,2,1,0:T(8,128)}, f32[24,256,256]{2,1,0:T(8,128)}) custom-call(f32[4,15,64,640]{3,2,1,0:T(8,128)} %bitcast.35), custom_call_target="tpu_custom_call" | custom-call | tf_op jit(solution)/shard_map/cond/branch_1_fun/pallas_call | solution.py:275
  307.0 15.2 %shard_map.38 = bf16[1,12,256,1280]{3,2,1,0:T(8,128)(2,1)} custom-call(s32[12]{0:T(128)S(1)} %gather_fusion, s32[12]{0:T(128)S(1)} %dynamic-slice_convert_fusion.valid_ref, s32[1]{0:T(128)} %bitcast.20.island_ref, f32[24,256,256]{2,1,0:T(8,128)} %get-tuple-element.104.m_ref, f32[24,256,640]{2,1,0:T(8,128)} %get-tuple-element.105.a_ref, ...), custom_call_target="tpu_custom_call" | custom-call | tf_op jit(solution)/shard_map/pallas_call | solution.py:322
  (1 shorter events, 0.0 us)
